TPU v7x, 512 devices: a whole 4x8x8 slice. The times are simulated.
512 devices in a mesh: dp: 8 (over x, y_hi), seq: 64 (over z, y_lo, core).
Axes of the slice: x: 4, y: 8 (y_hi: 2, y_lo: 4; y = y_hi * 4 + y_lo), z: 8, core: 2. Of those that a mesh axis runs over, the one named last changes fastest.
Arguments:
- points: bfloat16 [8, 16384, 384], P('dp', 'seq'), may hold values from -6 to 6
- cotangent: bfloat16 [8, 16384, 384], P('dp', 'seq'), may hold values from -6 to 6
- in_gain: float32 [384], replicated, may hold values from 0.5 to 2
- out_gain: float32 [384], replicated, may hold values from 0.5 to 2
- left_factor: bfloat16 [256, 256], replicated, may hold values from -0.375 to 0.375
- right_factor: bfloat16 [64, 64], replicated, may hold values from -0.75 to 0.75
- norm_gain: float32 [384], replicated, may hold values from 0.5 to 2
- gate_weight: bfloat16 [4, 96, 384], P(None, None, 'dp'), may hold values from -0.625 to 0.625
- up_weight: bfloat16 [4, 96, 384], P(None, None, 'dp'), may hold values from -0.625 to 0.625
- down_weight: bfloat16 [4, 96, 384], P(None, None, 'dp'), may hold values from -0.3125 to 0.3125
Outputs:
- layer_out: bfloat16 [8, 16384, 384], P('dp', 'seq')
- grad_points: bfloat16 [8, 16384, 384], P('dp', 'seq')
- grad_left: float32 [256, 256], replicated
- grad_right: float32 [64, 64], replicated
- grad_in_gain: float32 [384], replicated
- grad_out_gain: float32 [384], replicated
- grad_norm_gain: float32 [384], replicated
- grad_gate: float32 [4, 96, 384], P(None, None, 'dp')
- grad_up: float32 [4, 96, 384], P(None, None, 'dp')
- grad_down: float32 [4, 96, 384], P(None, None, 'dp')
All inputs are finite; a program needn't handle non-finite values.
Results may differ from a plain program's by a relative error of at most 0.0091.
Values may be sent and summed in bfloat16 or wider, within the bound.
A program may use at most 64 MiB of HBM per device.

v0:
```python
import jax
import jax.numpy as jnp
from jax import lax
from jax.sharding import PartitionSpec as P


def shards(
    points,
    cotangent,
    in_gain,
    out_gain,
    left_factor,
    right_factor,
    norm_gain,
    gate_weight,
    up_weight,
    down_weight,
):
    seq_count = lax.axis_size("seq")
    data_count = lax.axis_size("dp")
    row_count = points.shape[1]
    channels = points.shape[2]
    block_size = left_factor.shape[0]
    block_total = right_factor.shape[0]
    blocks = row_count // block_size
    shard_width = gate_weight.shape[2]
    gate_full, up_full, down_full = (
        lax.all_gather(gate_weight, "dp", axis=2, tiled=True),
        lax.all_gather(up_weight, "dp", axis=2, tiled=True),
        lax.all_gather(down_weight, "dp", axis=2, tiled=True),
    )
    nblocks = gate_full.shape[0]
    block_in = gate_full.shape[1]
    block_hidden = gate_full.shape[2]
    quarter = block_hidden // nblocks
    inputs = points[0].astype(jnp.float32)
    scaled = (inputs * in_gain).astype(jnp.bfloat16).reshape(blocks, block_size, channels)
    first_mix = jnp.einsum(
        "pb,abc->apc", left_factor, scaled, preferred_element_type=jnp.float32
    ).astype(jnp.bfloat16)
    received = lax.all_to_all(first_mix, "seq", split_axis=1, concat_axis=0, tiled=True)
    mixed = jnp.einsum("qa,apc->pqc", right_factor, received, preferred_element_type=jnp.float32)
    first_moved = received
    mixed = mixed.reshape(row_count, channels)
    residual = inputs + out_gain * mixed
    inv_rms = lax.rsqrt(jnp.mean(residual * residual, axis=-1, keepdims=True) + 1e-05)
    normed = residual * inv_rms
    hidden_in = (normed * norm_gain).astype(jnp.bfloat16).reshape(row_count, nblocks, block_in)
    gate_pre = jnp.einsum("rkd,kdf->rkf", hidden_in, gate_full, preferred_element_type=jnp.float32)
    up_pre = jnp.einsum("rkd,kdf->rkf", hidden_in, up_full, preferred_element_type=jnp.float32)
    sig_gate = jax.nn.sigmoid(gate_pre)
    act_gate = gate_pre * sig_gate
    hidden = (act_gate * up_pre).astype(jnp.bfloat16)
    hidden_grid = hidden.reshape(row_count, nblocks, nblocks, quarter)
    down_grid = down_full.reshape(nblocks, block_in, nblocks, quarter)
    branch = jnp.einsum(
        "rkjf,jokf->rjo", hidden_grid, down_grid, preferred_element_type=jnp.float32
    ).reshape(row_count, channels)
    layer_out = (residual + branch).astype(jnp.bfloat16)
    grad_grid = cotangent[0].reshape(row_count, nblocks, block_in)
    dhidden = jnp.einsum(
        "rjo,jokf->rkjf", grad_grid, down_grid, preferred_element_type=jnp.float32
    ).reshape(row_count, nblocks, block_hidden)
    grad_down = jnp.einsum(
        "rjo,rkjf->jokf", grad_grid, hidden_grid, preferred_element_type=jnp.float32
    ).reshape(nblocks, block_in, block_hidden)
    dgate = (dhidden * up_pre * sig_gate * (1.0 + gate_pre * (1.0 - sig_gate))).astype(jnp.bfloat16)
    dupper = (dhidden * act_gate).astype(jnp.bfloat16)
    dhid_in = jnp.einsum("rkf,kdf->rkd", dgate, gate_full, preferred_element_type=jnp.float32)
    dhid_in = (
        dhid_in + jnp.einsum("rkf,kdf->rkd", dupper, up_full, preferred_element_type=jnp.float32)
    ).reshape(row_count, channels)
    grad_gate = jnp.einsum("rkd,rkf->kdf", hidden_in, dgate, preferred_element_type=jnp.float32)
    grad_up = jnp.einsum("rkd,rkf->kdf", hidden_in, dupper, preferred_element_type=jnp.float32)
    grad_norm = jnp.sum(dhid_in * normed, axis=0)
    scaled_grad = dhid_in * norm_gain
    dresid = cotangent[0].astype(jnp.float32) + inv_rms * (
        scaled_grad - normed * jnp.mean(scaled_grad * normed, axis=-1, keepdims=True)
    )
    grad_out = jnp.sum(dresid * mixed, axis=0)
    dmixed = (
        (dresid * out_gain)
        .astype(jnp.bfloat16)
        .reshape(block_size // seq_count, block_total, channels)
    )
    dfirst = jnp.einsum(
        "qa,pqc->apc", right_factor, dmixed, preferred_element_type=jnp.float32
    ).astype(jnp.bfloat16)
    grad_right = jnp.einsum("pqc,apc->qa", dmixed, first_moved, preferred_element_type=jnp.float32)
    received = lax.all_to_all(dfirst, "seq", split_axis=0, concat_axis=1, tiled=True)
    dscaled = jnp.einsum("pb,apc->abc", left_factor, received, preferred_element_type=jnp.float32)
    grad_left = jnp.einsum("apc,abc->pb", received, scaled, preferred_element_type=jnp.float32)
    dscaled = dscaled.reshape(row_count, channels)
    grad_in = jnp.sum(dscaled * inputs, axis=0)
    grad_points = (dresid + dscaled * in_gain).astype(jnp.bfloat16)
    factor = float(data_count * row_count * seq_count) ** (-0.5)
    totals = lax.psum(
        (grad_gate, grad_up, grad_down, grad_left, grad_right, grad_in, grad_out, grad_norm),
        ("dp", "seq"),
    )
    start = lax.axis_index("dp") * shard_width
    gate_sum = lax.dynamic_slice_in_dim(totals[0], start, shard_width, 2)
    up_sum = lax.dynamic_slice_in_dim(totals[1], start, shard_width, 2)
    down_sum = lax.dynamic_slice_in_dim(totals[2], start, shard_width, 2)
    left_sum, right_sum, in_sum, out_sum, norm_sum = (
        totals[3],
        totals[4],
        totals[5],
        totals[6],
        totals[7],
    )
    return (
        layer_out[None],
        grad_points[None],
        left_sum * factor,
        right_sum * factor,
        in_sum * factor,
        out_sum * factor,
        norm_sum * factor,
        gate_sum * factor,
        up_sum * factor,
        down_sum * factor,
    )


def solution(mesh):
    in_specs = (
        P("dp", "seq", None),
        P("dp", "seq", None),
        P(),
        P(),
        P(),
        P(),
        P(),
        P(None, None, "dp"),
        P(None, None, "dp"),
        P(None, None, "dp"),
    )
    out_specs = (
        P("dp", "seq", None),
        P("dp", "seq", None),
        P(),
        P(),
        P(),
        P(),
        P(),
        P(None, None, "dp"),
        P(None, None, "dp"),
        P(None, None, "dp"),
    )
    return jax.shard_map(shards, mesh=mesh, in_specs=in_specs, out_specs=out_specs, check_vma=False)
```

profile of v0, /device:TPU:17, one launch (start us, length us, event | category | flops | bytes accessed | tf_op | source)
XLA Modules:
  0.0 500.2 jit_solution(1939229281374899762)
XLA Ops:
  7.2 0.9 copy-done
  8.1 1.2 fusion.8
  10.3 1.8 reduce.5
  12.1 0.8 reshape.326
  12.9 14.7 %all-to-all-start = ((bf16[64,2,768]{2,1,0:T(2,128)(2,1)}), bf16[64,2,768]{2,1,0:T(2,128)(2,1)}, u32[]{:S(2)}, u32[]{:S(2)}) async-start(bf16[64,2,768]{2,1,0:T(2,128)(2,1)} %reshape.326), calls=%async_computation | async-start | bytes 393216 | tf_op jit(solution)/shard_map/all_to_all | solution.py:41
  27.6 42.0 %all_gather.11 = bf16[4,96,384]{1,2,0:T(8,128)(2,1)S(1)} all-gather(bf16[4,96,48]{1,2,0:T(8,128)(2,1)S(1)} %copy-done.15), channel_id=1, replica_groups=mesh['dp'=8,'seq'=64] {'dp'}, dimensions={2}, use_global_device_ids=true | all-gather | bytes 331776 | tf_op jit(solution)/shard_map/all_gather | solution.py:30
  70.2 0.9 copy.60
  71.1 0.8 convert_element_type.81
  72.2 1.6 copy.69
  73.8 38.9 %all_gather.10 = bf16[4,96,384]{1,2,0:T(8,128)(2,1)S(1)} all-gather(bf16[4,96,48]{1,2,0:T(8,128)(2,1)S(1)} %copy-done.16), channel_id=1, replica_groups=mesh['dp'=8,'seq'=64] {'dp'}, dimensions={2}, use_global_device_ids=true | all-gather | bytes 331776 | tf_op jit(solution)/shard_map/all_gather | solution.py:29
  112.7 40.8 %all_gather.9 = bf16[4,96,384]{1,2,0:T(8,128)(2,1)S(1)} all-gather(bf16[4,96,48]{1,2,0:T(8,128)(2,1)S(1)} %copy-done.17), channel_id=1, replica_groups=mesh['dp'=8,'seq'=64] {'dp'}, dimensions={2}, use_global_device_ids=true | all-gather | bytes 331776 | tf_op jit(solution)/shard_map/all_gather | solution.py:28
  153.6 1.5 reshape.327
  155.1 1.1 bitcast_reduce_fusion
  157.9 0.8 copy-done.8
  158.7 2.0 multiply_convert_fusion
  161.1 1.3 fusion.32
  162.4 1.3 fusion.33
  164.2 0.9 copy.71
  165.8 0.9 copy.65
  167.4 1.2 multiply_reduce_fusion.1
  168.9 0.8 copy.74
  169.7 25.1 %all-to-all-start.1 = ((bf16[64,4,384]{2,1,0:T(4,128)(2,1)}), bf16[64,4,384]{2,1,0:T(4,128)(2,1)S(1)}, u32[]{:S(2)}, u32[]{:S(2)}) async-start(bf16[64,4,384]{2,1,0:T(4,128)(2,1)} %copy.74), calls=%async_computation.1 | async-start | bytes 393216 | tf_op jit(solution)/shard_map/all_to_all | solution.py:90
  195.2 1.2 fusion.10
  196.4 8.6 %all-to-all-done.1 = bf16[64,4,384]{2,1,0:T(4,128)(2,1)S(1)} async-done(((bf16[64,4,384]{2,1,0:T(4,128)(2,1)}), bf16[64,4,384]{2,1,0:T(4,128)(2,1)S(1)}, u32[]{:S(2)}, u32[]{:S(2)}) %all-to-all-start.1) | async-done | bytes 196640 | tf_op jit(solution)/shard_map/all_to_all | solution.py:90
  205.1 1.0 fusion.25
  206.2 1.0 fusion.18
  207.3 98.6 %all-reduce = (f32[64,64]{1,0:T(8,128)S(1)}, f32[384]{0:T(512)S(1)}, f32[384]{0:T(512)S(1)}, f32[384]{0:T(512)S(1)}) all-reduce(f32[64,64]{1,0:T(8,128)S(1)} %convolution_bitcast_fusion.1, f32[384]{0:T(512)S(1)} %fusion.12, f32[384]{0:T(512)S(1)} %get-tuple-element.20, ...), channel_id=1, replica_groups=mesh['dp'=8,'seq'=64] {'dp','seq'}, use_global_device_ids=true, to_apply=%region_3.0 | all-reduce | flops 5248 | bytes 41984 | tf_op jit(solution)/shard_map/psum | solution.py:97
  307.0 0.6 broadcast_multiply_fusion.1
  307.7 180.8 %all-reduce.4.cloned.1.call-done = (f32[256,256]{1,0:T(8,128)}, f32[4,96,384]{1,2,0:T(8,128)}, f32[4,96,384]{1,2,0:T(8,128)}, f32[4,96,384]{1,2,0:T(8,128)}) async-done(((f32[256,256]{1,0:T(8,128)}, f32[4,96,384]{1,2,0:T(8,128)}, f32[4,96,384]{1,2,0:T(8,128)}, f32[4,96,384]{1,2,0:T(8,128)}), (f32[256,256]{1,0:T(8,128)}, f32[4,96,384]{1,2,0:T(8,128)}, f32[4,96,384]{1,2,0:T(8,128)}, ...) | async-done | bytes 2031632 | tf_op jit(solution)/shard_map/psum | solution.py:97
  488.5 1.7 broadcast_multiply_fusion
  490.2 1.5 dynamic-slice_multiply_fusion.2
  491.7 1.6 dynamic-slice_multiply_fusion
  (72 shorter events, 7.5 us)
Async XLA Ops:
  7.2 0.9 copy-start
  7.2 20.4 %copy-start.15 = (bf16[4,96,48]{1,2,0:T(8,128)(2,1)S(1)}, bf16[4,96,48]{1,2,0:T(8,128)(2,1)}, u32[]{:S(2)}) copy-start(bf16[4,96,48]{1,2,0:T(8,128)(2,1)} %param.19) | copy-start | bytes 110596
  7.2 62.4 %copy-start.6 = (bf16[1,256,384]{2,1,0:T(8,128)(2,1)S(1)}, bf16[1,256,384]{2,1,0:T(8,128)(2,1)}, u32[]{:S(2)}) copy-start(bf16[1,256,384]{2,1,0:T(8,128)(2,1)} %param.11) | copy-start | bytes 589828
  12.9 140.7 %all-to-all-start = ((bf16[64,2,768]{2,1,0:T(2,128)(2,1)}), bf16[64,2,768]{2,1,0:T(2,128)(2,1)}, u32[]{:S(2)}, u32[]{:S(2)}) async-start(bf16[64,2,768]{2,1,0:T(2,128)(2,1)} %reshape.326), calls=%async_computation | async-start | bytes 393216 | tf_op jit(solution)/shard_map/all_to_all | solution.py:41
  27.6 42.6 %copy-start.1 = (bf16[1,256,384]{2,1,0:T(8,128)(2,1)S(1)}, bf16[1,256,384]{2,1,0:T(8,128)(2,1)}, u32[]{:S(2)}) copy-start(bf16[1,256,384]{2,1,0:T(8,128)(2,1)} %param.10) | copy-start | bytes 589828
  69.6 1.4 copy-start.2
  69.8 2.1 copy-start.4
  69.8 2.1 copy-start.19
  69.8 2.1 copy-start.13
  72.2 1.7 copy-start.16
  72.2 40.5 %copy-start.17 = (bf16[4,96,48]{1,2,0:T(8,128)(2,1)S(1)}, bf16[4,96,48]{1,2,0:T(8,128)(2,1)}, u32[]{:S(2)}) copy-start(bf16[4,96,48]{1,2,0:T(8,128)(2,1)} %param.17) | copy-start | bytes 110596
  73.8 82.5 %copy-start.14 = (bf16[64,64]{1,0:T(8,128)(2,1)S(1)}, bf16[64,64]{1,0:T(8,128)(2,1)}, u32[]{:S(2)}) copy-start(bf16[64,64]{1,0:T(8,128)(2,1)} %param.15) | copy-start | bytes 24580
  156.3 1.0 copy-start.9
  157.3 1.4 copy-start.8
  163.7 1.5 copy-start.12
  164.2 1.2 copy-start.3
  165.8 1.5 copy-start.7
  167.3 27.8 %copy-start.5 = (bf16[1,256,384]{1,2,0:T(8,128)(2,1)S(1)}, bf16[1,256,384]{1,2,0:T(8,128)(2,1)}, u32[]{:S(2)}) copy-start(bf16[1,256,384]{1,2,0:T(8,128)(2,1)} %copy-done.4) | copy-start | bytes 589828
  169.7 35.3 %copy-start.18 = (f32[384]{0:T(512)S(1)}, f32[384]{0:T(512)}, u32[]{:S(2)}) copy-start(f32[384]{0:T(512)} %param.12) | copy-start | bytes 4612
  169.7 35.3 %all-to-all-start.1 = ((bf16[64,4,384]{2,1,0:T(4,128)(2,1)}), bf16[64,4,384]{2,1,0:T(4,128)(2,1)S(1)}, u32[]{:S(2)}, u32[]{:S(2)}) async-start(bf16[64,4,384]{2,1,0:T(4,128)(2,1)} %copy.74), calls=%async_computation.1 | async-start | bytes 393216 | tf_op jit(solution)/shard_map/all_to_all | solution.py:90
  194.8 293.7 %all-reduce.4.cloned.1.call-start = ((), (), s32[]{:S(2)}) async-start(), calls=%async_computation.2 | async-start | bytes 5242880 | tf_op jit(solution)/shard_map/psum | solution.py:97
  205.0 1.0 copy-start.10
  205.1 1.1 copy-start.11
Sparse Core Ops, SparseCore 0:
  206.2 282.2 all-reduce.3
where the time goes:
time: 501 us; the launch traced here: 500 us
  blocking collectives  220 us (44%)
  waiting for transfers between devices  189 us (38%)
  starting transfers between devices  39.9 us (8%)
  between operations  14.4 us (3%)
  local copies, waits for them, and re-layouts  13.6 us (3%)
  matrix products  11.6 us (2%)
  other arithmetic  10.9 us (2%)
    psum x1, waiting for transfers between devices, shards(): lax.psum((grad_gate, grad_up, grad_down, grad_left, grad_right, grad_in,...  181 us
    psum x1, blocking collectives, shards(): lax.psum((grad_gate, grad_up, grad_down, grad_left, grad_right, grad_in,...  98.6 us
    all_gather x1, blocking collectives, shards(): lax.all_gather(down_weight, 'dp', axis=2, tiled=True)  42 us
    all_gather x1, blocking collectives, shards(): lax.all_gather(gate_weight, 'dp', axis=2, tiled=True)  40.8 us
    all_gather x1, blocking collectives, shards(): lax.all_gather(up_weight, 'dp', axis=2, tiled=True)  38.9 us
    all_to_all x1, starting transfers between devices, shards(): lax.all_to_all(dfirst, 'seq', split_axis=0, concat_axis=1, tiled=True)  25.1 us
    all_to_all x1, starting transfers between devices, shards(): lax.all_to_all(first_mix, 'seq', split_axis=1, concat_axis=0, tiled=True)  14.7 us
  transfers between devices with their start and end apart: 3, of which 2 were waited for; matrix products, arithmetic and copies ran while one was open for 2% of the time, Pallas kernels for 0%

commit v1 on v0

--- a/solution.py
+++ b/solution.py
@@ -25,7 +25,9 @@
     blocks = row_count // block_size
     shard_width = gate_weight.shape[2]
     gate_full, up_full, down_full = (
-        lax.all_gather(gate_weight, "dp", axis=2, tiled=True),
+        jnp.concatenate(
+            lax.all_to_all(jnp.stack([gate_weight] * lax.axis_size("dp")), "dp", 0, 0), axis=2
+        ),
         lax.all_gather(up_weight, "dp", axis=2, tiled=True),
         lax.all_gather(down_weight, "dp", axis=2, tiled=True),
     )

time: 501 us -> 471 us (0.940)
  blocking collectives: 220 us -> 176 us
  starting transfers between devices: 39.9 us -> 46.2 us
    all_gather x1 -> x0, blocking collectives: 40.8 us -> none  [shards(): lax.all_gather(gate_weight, 'dp', axis=2, tiled=True)]
    all_to_all x0 -> x1, starting transfers between devices: none -> 6.61 us  [shards(): lax.all_to_all(jnp.stack([gate_weight] * lax.axis_size('dp')), 'dp', 0, 0)]
    all_to_all x0 -> x1, waiting for transfers between devices: none -> 5.88 us  [shards(): lax.all_to_all(jnp.stack([gate_weight] * lax.axis_size('dp')), 'dp', 0, 0)]
  transfers between devices with their start and end apart: 3 -> 4, of which waited for: 2 -> 3; matrix products, arithmetic and copies ran while one was open for 2% -> 3% of each run, Pallas kernels for 0% -> 0%
where the time goes in v1:
time: 471 us; the launch traced here: 470 us
  waiting for transfers between devices  194 us (41%)
  blocking collectives  176 us (37%)
  starting transfers between devices  46.2 us (10%)
  matrix products  14.6 us (3%)
  between operations  14.3 us (3%)
  local copies, waits for them, and re-layouts  13.3 us (3%)
  other arithmetic  12.5 us (3%)
    psum x1, waiting for transfers between devices, shards(): lax.psum((grad_gate, grad_up, grad_down, grad_left, grad_right, grad_in,...  179 us
    psum x1, blocking collectives, shards(): lax.psum((grad_gate, grad_up, grad_down, grad_left, grad_right, grad_in,...  95 us
    all_gather x1, blocking collectives, shards(): lax.all_gather(down_weight, 'dp', axis=2, tiled=True)  41.4 us
    all_gather x1, blocking collectives, shards(): lax.all_gather(up_weight, 'dp', axis=2, tiled=True)  39.2 us
    all_to_all x1, starting transfers between devices, shards(): lax.all_to_all(dfirst, 'seq', split_axis=0, concat_axis=1, tiled=True)  25 us
    all_to_all x1, starting transfers between devices, shards(): lax.all_to_all(first_mix, 'seq', split_axis=1, concat_axis=0, tiled=True)  14.5 us
  transfers between devices with their start and end apart: 4, of which 3 were waited for; matrix products, arithmetic and copies ran while one was open for 3% of the time, Pallas kernels for 0%

profile of v1, /device:TPU:17, one launch (start us, length us, event | category | flops | bytes accessed | tf_op | source)
XLA Modules:
  0.0 470.4 jit_solution(11790846292883125581)
XLA Ops:
  7.2 0.9 copy-done
  8.1 1.2 fusion.8
  10.3 1.8 reduce.5
  12.1 0.8 reshape.336
  12.9 14.5 %all-to-all-start = ((bf16[64,2,768]{2,1,0:T(2,128)(2,1)}), bf16[64,2,768]{2,1,0:T(2,128)(2,1)S(1)}, u32[]{:S(2)}, u32[]{:S(2)}) async-start(bf16[64,2,768]{2,1,0:T(2,128)(2,1)} %reshape.336), calls=%async_computation | async-start | bytes 393216 | tf_op jit(solution)/shard_map/all_to_all | solution.py:43
  27.5 0.9 copy.63
  29.3 41.4 %all_gather.7 = bf16[4,96,384]{1,2,0:T(8,128)(2,1)S(1)} all-gather(bf16[4,96,48]{1,2,0:T(8,128)(2,1)S(1)} %copy-done.8), channel_id=1, replica_groups=mesh['dp'=8,'seq'=64] {'dp'}, dimensions={2}, use_global_device_ids=true | all-gather | bytes 331776 | tf_op jit(solution)/shard_map/all_gather | solution.py:32
  71.4 1.6 copy.74
  73.0 39.2 %all_gather.6 = bf16[4,96,384]{1,2,0:T(8,128)(2,1)S(1)} all-gather(bf16[4,96,48]{1,2,0:T(8,128)(2,1)S(1)} %copy-done.9), channel_id=1, replica_groups=mesh['dp'=8,'seq'=64] {'dp'}, dimensions={2}, use_global_device_ids=true | all-gather | bytes 331776 | tf_op jit(solution)/shard_map/all_gather | solution.py:31
  113.0 6.6 %all-to-all-start.1 = ((bf16[8,4,96,48]{2,3,1,0:T(8,128)(2,1)}), bf16[8,4,96,48]{2,3,1,0:T(8,128)(2,1)S(1)}, u32[]{:S(2)}, u32[]{:S(2)}) async-start(bf16[8,4,96,48]{2,3,1,0:T(8,128)(2,1)} %stack.2), calls=%async_computation.1 | async-start | bytes 786432 | tf_op jit(solution)/shard_map/all_to_all | solution.py:29
  119.8 1.1 bitcast_reduce_fusion
  121.9 1.9 multiply_convert_fusion.2
  123.8 1.6 fusion.30
  125.4 5.9 %all-to-all-done.1 = bf16[8,4,96,48]{2,3,1,0:T(8,128)(2,1)S(1)} async-done(((bf16[8,4,96,48]{2,3,1,0:T(8,128)(2,1)}), bf16[8,4,96,48]{2,3,1,0:T(8,128)(2,1)S(1)}, u32[]{:S(2)}, u32[]{:S(2)}) %all-to-all-start.1) | async-done | bytes 294944 | tf_op jit(solution)/shard_map/all_to_all | solution.py:29
  131.3 3.8 multiply_convert_fusion
  135.5 1.3 fusion.32
  136.8 1.3 fusion.33
  138.7 0.9 copy.77
  139.6 1.4 copy.67
  141.3 0.9 copy.70
  142.8 1.2 multiply_reduce_fusion.1
  144.3 0.8 copy.80
  145.1 25.0 %all-to-all-start.2 = ((bf16[64,4,384]{2,1,0:T(4,128)(2,1)}), bf16[64,4,384]{2,1,0:T(4,128)(2,1)S(1)}, u32[]{:S(2)}, u32[]{:S(2)}) async-start(bf16[64,4,384]{2,1,0:T(4,128)(2,1)} %copy.80), calls=%async_computation.2 | async-start | bytes 393216 | tf_op jit(solution)/shard_map/all_to_all | solution.py:92
  170.4 1.3 fusion.10
  171.7 8.6 %all-to-all-done.2 = bf16[64,4,384]{2,1,0:T(4,128)(2,1)S(1)} async-done(((bf16[64,4,384]{2,1,0:T(4,128)(2,1)}), bf16[64,4,384]{2,1,0:T(4,128)(2,1)S(1)}, u32[]{:S(2)}, u32[]{:S(2)}) %all-to-all-start.2) | async-done | bytes 196640 | tf_op jit(solution)/shard_map/all_to_all | solution.py:92
  180.3 1.0 fusion.25
  181.4 1.0 fusion.18
  182.5 95.0 %all-reduce = (f32[64,64]{1,0:T(8,128)S(1)}, f32[384]{0:T(512)S(1)}, f32[384]{0:T(512)S(1)}, f32[384]{0:T(512)S(1)}) all-reduce(f32[64,64]{1,0:T(8,128)S(1)} %convolution_bitcast_fusion.1, f32[384]{0:T(512)S(1)} %fusion.12, f32[384]{0:T(512)S(1)} %get-tuple-element.20, ...), channel_id=1, replica_groups=mesh['dp'=8,'seq'=64] {'dp','seq'}, use_global_device_ids=true, to_apply=%region_3.0 | all-reduce | flops 5248 | bytes 41984 | tf_op jit(solution)/shard_map/psum | solution.py:99
  279.3 179.4 %all-reduce.4.cloned.1.call-done = (f32[256,256]{1,0:T(8,128)}, f32[4,96,384]{1,2,0:T(8,128)}, f32[4,96,384]{1,2,0:T(8,128)}, f32[4,96,384]{1,2,0:T(8,128)}) async-done(((f32[256,256]{1,0:T(8,128)}, f32[4,96,384]{1,2,0:T(8,128)}, f32[4,96,384]{1,2,0:T(8,128)}, f32[4,96,384]{1,2,0:T(8,128)}), (f32[256,256]{1,0:T(8,128)}, f32[4,96,384]{1,2,0:T(8,128)}, f32[4,96,384]{1,2,0:T(8,128)}, ...) | async-done | bytes 2031632 | tf_op jit(solution)/shard_map/psum | solution.py:99
  458.7 1.7 broadcast_multiply_fusion
  460.4 1.5 dynamic-slice_multiply_fusion.2
  461.9 1.6 dynamic-slice_multiply_fusion
  (61 shorter events, 8.9 us)
Async XLA Ops:
  7.2 0.9 copy-start
  7.2 20.3 %copy-start.1 = (bf16[1,256,384]{2,1,0:T(8,128)(2,1)S(1)}, bf16[1,256,384]{2,1,0:T(8,128)(2,1)}, u32[]{:S(2)}) copy-start(bf16[1,256,384]{2,1,0:T(8,128)(2,1)} %param.10) | copy-start | bytes 589828
  9.3 19.9 %copy-start.12 = (f32[384]{0:T(512)S(1)}, f32[384]{0:T(512)}, u32[]{:S(2)}) copy-start(f32[384]{0:T(512)} %param.16) | copy-start | bytes 4612
  9.3 19.9 %copy-start.6 = (f32[384]{0:T(512)S(1)}, f32[384]{0:T(512)}, u32[]{:S(2)}) copy-start(f32[384]{0:T(512)} %param.13) | copy-start | bytes 4612
  9.3 20.0 %copy-start.8 = (bf16[4,96,48]{1,2,0:T(8,128)(2,1)S(1)}, bf16[4,96,48]{1,2,0:T(8,128)(2,1)}, u32[]{:S(2)}) copy-start(bf16[4,96,48]{1,2,0:T(8,128)(2,1)} %param.19) | copy-start | bytes 110596
  9.8 61.0 %copy-start.2 = (bf16[1,256,384]{2,1,0:T(8,128)(2,1)S(1)}, bf16[1,256,384]{2,1,0:T(8,128)(2,1)}, u32[]{:S(2)}) copy-start(bf16[1,256,384]{2,1,0:T(8,128)(2,1)} %param.11) | copy-start | bytes 589828
  12.9 99.3 %all-to-all-start = ((bf16[64,2,768]{2,1,0:T(2,128)(2,1)}), bf16[64,2,768]{2,1,0:T(2,128)(2,1)S(1)}, u32[]{:S(2)}, u32[]{:S(2)}) async-start(bf16[64,2,768]{2,1,0:T(2,128)(2,1)} %reshape.336), calls=%async_computation | async-start | bytes 393216 | tf_op jit(solution)/shard_map/all_to_all | solution.py:43
  71.4 1.7 copy-start.9
  71.4 40.8 %copy-start.10 = (bf16[4,96,48]{1,2,0:T(8,128)(2,1)S(1)}, bf16[4,96,48]{1,2,0:T(8,128)(2,1)}, u32[]{:S(2)}) copy-start(bf16[4,96,48]{1,2,0:T(8,128)(2,1)} %param.17) | copy-start | bytes 110596
  73.0 47.9 %copy-start.7 = (bf16[64,64]{1,0:T(8,128)(2,1)S(1)}, bf16[64,64]{1,0:T(8,128)(2,1)}, u32[]{:S(2)}) copy-start(bf16[64,64]{1,0:T(8,128)(2,1)} %param.15) | copy-start | bytes 24580
  113.0 18.3 %all-to-all-start.1 = ((bf16[8,4,96,48]{2,3,1,0:T(8,128)(2,1)}), bf16[8,4,96,48]{2,3,1,0:T(8,128)(2,1)S(1)}, u32[]{:S(2)}, u32[]{:S(2)}) async-start(bf16[8,4,96,48]{2,3,1,0:T(8,128)(2,1)} %stack.2), calls=%async_computation.1 | async-start | bytes 786432 | tf_op jit(solution)/shard_map/all_to_all | solution.py:29
  135.5 2.7 copy-start.5
  145.1 35.2 %copy-start.11 = (f32[384]{0:T(512)S(1)}, f32[384]{0:T(512)}, u32[]{:S(2)}) copy-start(f32[384]{0:T(512)} %param.12) | copy-start | bytes 4612
  145.1 35.1 %all-to-all-start.2 = ((bf16[64,4,384]{2,1,0:T(4,128)(2,1)}), bf16[64,4,384]{2,1,0:T(4,128)(2,1)S(1)}, u32[]{:S(2)}, u32[]{:S(2)}) async-start(bf16[64,4,384]{2,1,0:T(4,128)(2,1)} %copy.80), calls=%async_computation.2 | async-start | bytes 393216 | tf_op jit(solution)/shard_map/all_to_all | solution.py:92
  170.1 288.6 %all-reduce.4.cloned.1.call-start = ((), (), s32[]{:S(2)}) async-start(), calls=%async_computation.3 | async-start | bytes 5242880 | tf_op jit(solution)/shard_map/psum | solution.py:99
  180.3 1.0 copy-start.3
  180.3 1.1 copy-start.4
Sparse Core Ops, SparseCore 0:
  181.4 277.2 all-reduce.3
